TPU v7x, 512 devices: a whole 4x4x16 slice. The times are simulated.
512 devices in a mesh: seq: 64 (over x, z), head: 8 (over y, core).
Axes of the slice: x: 4, y: 4, z: 16, core: 2. Of those that a mesh axis runs over, the one named last changes fastest.
Arguments:
- ssm_input: bfloat16 [16384, 8192], P('seq', 'head'), may hold values from -6 to 6
- bc_input: bfloat16 [16384, 2048], P('seq', 'head'), may hold values from -4 to 4
- conv_taps: float32 [4, 8192], P(None, 'head'), may hold values from -3 to 3
- conv_bias: float32 [8192], P('head'), may hold values from -1 to 0
- bc_taps: float32 [4, 2048], P(None, 'head'), may hold values from -3 to 3
- bc_bias: float32 [2048], P('head'), may hold values from -0.6 to 0.35
- step_input: float32 [128, 16384], P('head', 'seq'), may hold values from -4 to 4
- step_bias: float32 [128], P('head'), may hold values from -8 to -2
- decay_log: float32 [128], P('head'), may hold values from -8 to -1
- skip_gain: float32 [128], P('head'), may hold values from 0.5 to 2
- request_offset: int32 [16384], P('seq'), may hold values from 0 to 8191, as said below
Outputs:
- ssm_output: bfloat16 [16384, 8192], P('seq', 'head')
Inputs may be any that keep to these rules, and one draw needn't show every extreme that they name: request_offset counts the earlier tokens of the token's request: 0 at the first token and wherever a request starts, else one more than at the token before; one request has exactly 8192 tokens and none has more.
All inputs are finite; a program needn't handle non-finite values.
Results may differ from a plain program's by a relative error of at most 0.0095.
Values may be sent and summed in bfloat16 or wider, within the bound.
A program may use at most 192 MiB of HBM per device.

v0:
```python
import jax
import jax.numpy as jnp
from jax import lax
from jax.sharding import PartitionSpec as P

HEADDIM = 64
BLOCK = 256


def passed_along(block, axis, distance):
    devices = range(lax.axis_size(axis))
    route = [(i - distance, i) for i in devices if i - distance in devices]
    return lax.ppermute(block, axis, route)


def from_partner(array, axis, stride):
    return lax.ppermute(array, axis, [(i, i ^ 1 << stride) for i in range(lax.axis_size(axis))])


def prefix(value, axis, join, neutral):
    count, mine = (lax.axis_size(axis), lax.axis_index(axis))
    pieces = jax.tree.map(lambda part: lax.all_gather(part, axis), value)
    total = jax.tree.map(
        lambda part, zero: jnp.full_like(part, 0) + jnp.asarray(zero, part.dtype), value, neutral
    )

    def hop(position, total):
        longer = join(total, jax.tree.map(lambda part: part[position], pieces))
        return jax.tree.map(lambda new, old: jnp.where(position < mine, new, old), longer, total)

    return lax.fori_loop(0, count - 1, hop, total)


def conv_silu(source, earlier, tap_weights, tap_bias, offset):
    tok_rows = source.shape[0]
    tap_count = tap_weights.shape[0]
    extended = jnp.concatenate([earlier, source], axis=0)
    summed = jnp.zeros(source.shape, jnp.float32) + tap_bias[None, :]
    for lag_steps in range(tap_count):
        first_row = tap_count - 1 - lag_steps
        shifted = extended[first_row : first_row + tok_rows].astype(jnp.float32)
        in_request = (offset >= lag_steps).astype(jnp.float32)[:, None]
        summed = summed + tap_weights[tap_count - 1 - lag_steps][None, :] * shifted * in_request
    return jax.nn.silu(summed).astype(jnp.bfloat16)


def block_terms(x_block, b_block, c_block, step_block, decay_block, offset_block):
    block_len = offset_block.shape[0]
    rate_sum = jnp.cumsum(decay_block, axis=1)
    positions = lax.iota(jnp.int32, block_len)
    linked = (positions[None, :] <= positions[:, None]) & (
        offset_block[:, None] >= positions[:, None] - positions[None, :]
    )
    scores = jnp.einsum("in,jn->ij", c_block, b_block, preferred_element_type=jnp.float32)
    rate_gap = jnp.where(linked[None], rate_sum[:, :, None] - rate_sum[:, None, :], -1e30)
    weights = (scores[None] * jnp.exp(rate_gap) * step_block[:, None, :]).astype(jnp.bfloat16)
    intra_part = jnp.einsum("hij,jhp->ihp", weights, x_block, preferred_element_type=jnp.float32)
    tail_gap = jnp.where(
        offset_block[-1] >= block_len - 1 - positions[None, :], rate_sum[:, -1:] - rate_sum, -1e30
    )
    weighted_b = (
        b_block[None].astype(jnp.float32) * (jnp.exp(tail_gap) * step_block)[:, :, None]
    ).astype(jnp.bfloat16)
    block_state = jnp.einsum(
        "hjn,jhp->hnp", weighted_b, x_block, preferred_element_type=jnp.float32
    )
    carry_scale = jnp.exp(rate_sum) * (offset_block >= positions + 1).astype(jnp.float32)[None, :]
    passing = jnp.exp(rate_sum[:, -1]) * (offset_block[-1] >= block_len).astype(jnp.float32)
    return (intra_part, block_state, carry_scale, passing)


def state_read(c_float, state_value):
    return jnp.einsum("in,hnp->ihp", c_float, state_value, precision=lax.Precision.HIGHEST)


def combine(earlier, latter):
    return (earlier[0] * latter[0], latter[0][:, None, None] * earlier[1] + latter[1])


def on_device(
    ssm_input,
    bc_input,
    conv_taps,
    conv_bias,
    bc_taps,
    bc_bias,
    step_input,
    step_bias,
    decay_log,
    skip_gain,
    request_offset,
):
    tok_rows = ssm_input.shape[0]
    tap_count = conv_taps.shape[0]
    head_count = step_input.shape[0]
    state_size = bc_input.shape[1]
    earlier_x, earlier_bc = passed_along(
        (ssm_input[tok_rows - tap_count + 1 :], bc_input[tok_rows - tap_count + 1 :]), "seq", 1
    )
    x_conv = conv_silu(ssm_input, earlier_x, conv_taps, conv_bias, request_offset)
    own_half = conv_silu(bc_input, earlier_bc, bc_taps, bc_bias, request_offset)
    partner = from_partner(own_half, "head", 0)
    is_even = lax.axis_index("head") % 2 == 0
    b_rows = jnp.where(is_even, own_half, partner)
    c_rows = jnp.where(is_even, partner, own_half)
    time_step = jax.nn.softplus(step_input + step_bias[:, None])
    log_decay = -jnp.exp(decay_log)[:, None] * time_step
    block_count = tok_rows // BLOCK
    x_blocks = x_conv.reshape(block_count, BLOCK, head_count, HEADDIM)
    block_number = 0
    pieces = [
        block_terms(x_blocks[block_number], b_rows, c_rows, time_step, log_decay, request_offset)
    ]
    run_state = jnp.zeros((head_count, state_size, HEADDIM), jnp.float32)
    decay_prefix = jnp.ones((head_count,), jnp.float32)
    intra_part, block_state, carry_scale, passing = pieces[0]
    entering = [run_state]
    before = [decay_prefix]
    run_state = passing[:, None, None] * run_state + block_state
    decay_prefix = decay_prefix * passing
    identity = (jnp.ones_like(decay_prefix), jnp.zeros_like(run_state))
    totals, carry_in = prefix((decay_prefix, run_state), "seq", combine, identity)
    block_number = 0
    intra_part, block_state, carry_scale, passing = pieces[block_number]
    c_float = c_rows.astype(jnp.float32)
    x_float = x_blocks[block_number].astype(jnp.float32)
    incoming = before[block_number][:, None, None] * carry_in
    inter_part = state_read(c_float, entering[block_number] + incoming)
    block_out = (
        intra_part + inter_part * carry_scale.T[:, :, None] + skip_gain[None, :, None] * x_float
    )
    outputs = block_out.reshape(BLOCK, head_count * HEADDIM).astype(jnp.bfloat16)
    return outputs


def solution(mesh):
    return jax.shard_map(
        on_device,
        mesh=mesh,
        in_specs=(
            P("seq", "head"),
            P("seq", "head"),
            P(None, "head"),
            P("head"),
            P(None, "head"),
            P("head"),
            P("head", "seq"),
            P("head"),
            P("head"),
            P("head"),
            P("seq"),
        ),
        out_specs=P("seq", "head"),
        check_vma=False,
    )
```

profile of v0, /device:TPU:1, one launch (start us, length us, event | category | flops | bytes accessed | tf_op | source)
XLA Modules:
  0.0 891.6 jit_solution(15166144032974948664)
XLA Ops:
  7.2 4.4 collective-permute-start.1
  12.3 3.5 collective-permute-start
  24.9 3.5 collective-permute-start.2
  35.9 118.0 %all-reduce = f32[1024]{0:T(1024)S(1)} all-reduce(f32[1024]{0:T(1024)S(1)} %dynamic-update-slice), channel_id=2, replica_groups=mesh['seq'=64,'head'=8] {'seq'}, use_global_device_ids=true, to_apply=%add | all-reduce | flops 1024 | bytes 8192
  155.0 395.9 %all-gather.4.cloned.1.call-done = f32[1024,256,64]{1,2,0:T(8,128)} async-done(((f32[16,256,64]{1,2,0:T(8,128)}), f32[1024,256,64]{1,2,0:T(8,128)}) %all-gather.4.cloned.1.call-update) | async-done | bytes 67108880 | tf_op jit(solution)/shard_map/all_gather | solution.py:22
  550.9 328.4 %while.14 = (s32[]{:T(128)}, f32[16,256,64]{2,1,0:T(8,128)}, s32[]{:T(128)}, f32[64,16]{1,0:T(8,128)S(1)}, f32[64,16,256,64]{2,3,1,0:T(8,128)}, /*index=5*/s32[]{:T(128)}, s32[]{:T(128)}) while((s32[]{:T(128)}, f32[16,256,64]{2,1,0:T(8,128)}, s32[]{:T(128)}, f32[64,16]{1,0:T(8,128)S(1)}, f32[64,16,256,64]{2,3,1,0:T(8,128)}, ...), condition=%wide.region_3.4_spmd.clone, body=%wide.region_2.3_spmd.clone.sunk | while | flops 1048580 | bytes 7340329 | solution.py:31
  556.5 3.3 fusion.28
  561.7 3.3 fusion.28
  567.0 3.3 fusion.28
  572.2 3.3 fusion.28
  577.4 3.3 fusion.28
  582.7 3.3 fusion.28
  587.9 3.3 fusion.28
  593.1 3.3 fusion.28
  598.4 3.3 fusion.28
  603.6 3.3 fusion.28
  608.9 3.3 fusion.28
  614.1 3.3 fusion.28
  619.3 3.3 fusion.28
  624.6 3.3 fusion.28
  629.8 3.3 fusion.28
  635.0 3.3 fusion.28
  640.3 3.3 fusion.28
  645.5 3.3 fusion.28
  650.8 3.3 fusion.28
  656.0 3.3 fusion.28
  661.2 3.3 fusion.28
  666.5 3.3 fusion.28
  671.7 3.3 fusion.28
  677.0 3.3 fusion.28
  682.2 3.3 fusion.28
  687.4 3.3 fusion.28
  692.7 3.3 fusion.28
  697.9 3.3 fusion.28
  703.1 3.3 fusion.28
  708.4 3.3 fusion.28
  713.6 3.3 fusion.28
  718.9 3.3 fusion.28
  724.1 3.3 fusion.28
  729.3 3.3 fusion.28
  734.6 3.3 fusion.28
  739.8 3.3 fusion.28
  745.0 3.3 fusion.28
  750.3 3.3 fusion.28
  755.5 3.3 fusion.28
  760.8 3.3 fusion.28
  766.0 3.3 fusion.28
  771.2 3.3 fusion.28
  776.5 3.3 fusion.28
  781.7 3.3 fusion.28
  786.9 3.3 fusion.28
  792.2 3.3 fusion.28
  797.4 3.3 fusion.28
  802.7 3.3 fusion.28
  807.9 3.3 fusion.28
  813.1 3.3 fusion.28
  818.4 3.3 fusion.28
  823.6 3.3 fusion.28
  828.9 3.3 fusion.28
  834.1 3.3 fusion.28
  839.3 3.3 fusion.28
  844.6 3.3 fusion.28
  849.8 3.3 fusion.28
  855.0 3.3 fusion.28
  (243 shorter events, 159.5 us)
Async XLA Ops:
  6.5 544.3 %all-gather.4.cloned.1.call-start = ((), (), s32[]{:S(2)}) async-start(), calls=%async_computation | async-start | bytes 68157440 | tf_op jit(solution)/shard_map/all_gather | solution.py:22
  7.2 16.3 %collective-permute-start.1 = (bf16[3,256]{1,0:T(4,128)(2,1)S(1)}, bf16[3,256]{1,0:T(4,128)(2,1)S(1)}, u32[]{:S(2)}, u32[]{:S(2)}) collective-permute-start(bf16[3,256]{1,0:T(4,128)(2,1)S(1)} %slice.72), channel_id=1, source_target_pairs={{0,8},{8,16},{16,24},{24,32},{32,40},{40,48},{48,56},{56,64},{64,7... | collective-permute-start | bytes 4616 | tf_op jit(solution)/shard_map/ppermute | solution.py:13
  12.3 16.1 %collective-permute-start = (bf16[3,1024]{1,0:T(4,128)(2,1)S(1)}, bf16[3,1024]{1,0:T(4,128)(2,1)S(1)}, u32[]{:S(2)}, u32[]{:S(2)}) collective-permute-start(bf16[3,1024]{1,0:T(4,128)(2,1)S(1)} %slice.64), channel_id=1, source_target_pairs={{0,8},{8,16},{16,24},{24,32},{32,40},{40,48},{48,56},{56,64},{64,7... | collective-permute-start | bytes 18440 | tf_op jit(solution)/shard_map/ppermute | solution.py:13
  24.9 6.8 collective-permute-start.2
  31.7 123.3 %copy-start = (bf16[256,1024]{0,1:T(8,128)(2,1)}, bf16[256,1024]{0,1:T(8,128)(2,1)S(1)}, u32[]{:S(2)}) copy-start(bf16[256,1024]{0,1:T(8,128)(2,1)S(1)} %copy.23) | copy-start | bytes 1572868
  31.8 122.2 %copy-start.3 = (s32[256]{0:T(256)S(1)}, s32[256]{0:T(256)}, u32[]{:S(2)}) copy-start(s32[256]{0:T(256)} %param.23) | copy-start | bytes 3076
  879.3 2.9 copy-start.1
  879.3 2.9 copy-start.2
  879.3 2.9 copy-start.4
Sparse Core Ops, SparseCore 0:
  33.8 516.9 all-gather.3
where the time goes:
time: 897 us; the launch traced here: 892 us
  waiting for transfers between devices  396 us (44%)
  other arithmetic  213 us (24%)
  local copies, waits for them, and re-layouts  131 us (15%)
  blocking collectives  118 us (13%)
  between operations  14.9 us (2%)
  starting transfers between devices  11.3 us (1%)
    all_gather x1, waiting for transfers between devices, prefix(): pieces = jax.tree.map(lambda part: lax.all_gather(part, axis), value)  396 us
    select_n x63, other arithmetic, hop(): jnp.where(position < mine, new, old)  205 us
    dynamic_slice x126, local copies, waits for them, and re-layouts, hop(): longer = join(total, jax.tree.map(lambda part: part[position], pieces))  121 us
    unnamed x1, blocking collectives  118 us
  transfers between devices with their start and end apart: 4, of which 1 were waited for; matrix products, arithmetic and copies ran while one was open for 2% of the time, Pallas kernels for 0%

commit v1 on v0

v1 whole, which is shorter than its diff:
```python
import functools

import jax
import jax.numpy as jnp
from jax import lax
from jax.experimental import pallas as pl
from jax.experimental.pallas import tpu as pltpu
from jax.sharding import PartitionSpec as P

HEADDIM = 64
LANES = 128
MESH = pl.DeviceIdType.MESH
F32 = jnp.float32
BF16 = jnp.bfloat16


def split3(value):
    high = value.astype(BF16)
    rest = value - high.astype(F32)
    mid = rest.astype(BF16)
    low = (rest - mid.astype(F32)).astype(BF16)
    return high, mid, low


def iota(shape, axis):
    return lax.broadcasted_iota(jnp.int32, shape, axis)


def silu(v):
    return v / (1.0 + jnp.exp(-v))


def kernel(
    nx, nz, nc,
    xin, bcin, taps, bias, bct, bcb, step, sbias, dlog, sgain, off,
    out,
    xf, xfb, xc, offb, sexp, rexp, rate, td, xhalo, bchalo, bown, bother, bsel, csel,
    smask, y, st, recv, eb, ent, pas_s, pas_r, pexp, tb, tr, ptot, ptr,
    fs, fr, rs, rr, ts, tsr, ps, pr, as_, ar, hs, hr,
):
    tok = xin.shape[0]
    chans = xin.shape[1]
    state = bcin.shape[1]
    heads = step.shape[0]
    width = chans // nc
    rows = state // nz
    s = lax.axis_index("seq")
    head = lax.axis_index("head")
    x = s // nz
    z = lax.rem(s, nz)
    count = nx * nz
    nxt = lax.rem(s + 1, count)
    prv = lax.rem(s + count - 1, count)
    partner = head + 1 - 2 * lax.rem(head, 2)

    barrier = pltpu.get_barrier_semaphore()

    def greet(seq_index, head_index):
        pl.semaphore_signal(barrier, inc=1, device_id=(seq_index, head_index), device_id_type=MESH)

    greet(nxt, head)
    greet(prv, head)
    greet(s, partner)

    @pl.loop(1, nz)
    def _(d):
        greet(x * nz + lax.rem(z + d, nz), head)

    @pl.loop(1, nx)
    def _(d):
        greet(lax.rem(x + d, nx) * nz + z, head)

    off_row = jnp.minimum(off[...], tok).astype(F32)
    eye = (iota((tok, tok), 0) == iota((tok, tok), 1)).astype(BF16)
    off_rows = jnp.broadcast_to(off_row, (LANES, tok)).astype(BF16)
    offb[...] = lax.dot_general(eye, off_rows, (((1,), (1,)), ((), ())), preferred_element_type=F32)
    off_last = off_row[:, tok - 1 : tok]

    eye_h = iota((heads, heads), 0) == iota((heads, heads), 1)

    def column(row):
        return jnp.sum(jnp.where(eye_h, jnp.broadcast_to(row, (heads, heads)), 0.0), axis=1, keepdims=True)

    time_step = jnp.log1p(jnp.exp(step[...] + column(sbias[...])))
    log_decay = -jnp.exp(column(dlog[...])) * time_step
    upper = (iota((tok, tok), 0) <= iota((tok, tok), 1)).astype(F32)
    rate_row = jnp.dot(log_decay, upper, precision=lax.Precision.HIGHEST, preferred_element_type=F32)
    rate[...] = rate_row
    td[...] = time_step
    rate_last = rate_row[:, tok - 1 : tok]
    position = iota((1, tok), 1).astype(F32)
    tail = off_last >= (tok - 1) - position
    s_row = jnp.where(tail, jnp.exp(rate_last - rate_row), 0.0) * time_step
    passing = jnp.where(off_last >= tok, jnp.exp(rate_last), 0.0)

    spread = (lax.rem(iota((3 * heads, chans), 0), heads) == iota((3 * heads, chans), 1) // HEADDIM).astype(BF16)

    def expand(value):
        return lax.dot_general(
            jnp.concatenate(split3(value), axis=0), spread, (((0,), (0,)), ((), ())), preferred_element_type=F32
        )

    sexp[...] = expand(s_row)
    rexp[...] = expand(rate_row)

    def as_row(col):
        return jnp.sum(
            jnp.where(iota((heads, LANES), 0) == iota((heads, LANES), 1), jnp.broadcast_to(col, (heads, LANES)), 0.0),
            axis=0,
            keepdims=True,
        )

    pas_s[...] = jnp.broadcast_to(as_row(passing), (8, LANES))
    pas_r[pl.ds(z, 1)] = pas_s[...][None]

    def halo_copy(which):
        src = (xin, bcin)[which].at[pl.ds(tok - 16, 16), :]
        dst = (xhalo, bchalo)[which]
        return pltpu.make_async_remote_copy(
            src, dst, hs.at[which], hr.at[which], device_id=(nxt, head), device_id_type=MESH
        )

    def partner_copy():
        return pltpu.make_async_remote_copy(
            bown, bother, hs.at[2], hr.at[2], device_id=(s, partner), device_id_type=MESH
        )

    def pas_copy(d):
        to = x * nz + lax.rem(z + d, nz)
        return pltpu.make_async_remote_copy(
            pas_s, pas_r.at[z], as_.at[d], ar.at[d], device_id=(to, head), device_id_type=MESH
        )

    def fwd_copy(c, d):
        to = lax.rem(z + d, nz)
        return pltpu.make_async_remote_copy(
            st.at[c, to], recv.at[c, z], fs.at[c, d], fr.at[c, d], device_id=(x * nz + to, head), device_id_type=MESH
        )

    def ret_copy(c, d):
        to = lax.rem(z + d, nz)
        return pltpu.make_async_remote_copy(
            eb.at[c, to], ent.at[c, z], rs.at[c, d], rr.at[c, d], device_id=(x * nz + to, head), device_id_type=MESH
        )

    def total_copy(c, d):
        to = lax.rem(x + d, nx) * nz + z
        return pltpu.make_async_remote_copy(
            tb.at[c], tr.at[c, x], ts.at[c, d], tsr.at[c, d], device_id=(to, head), device_id_type=MESH
        )

    def ptot_copy(d):
        to = lax.rem(x + d, nx) * nz + z
        return pltpu.make_async_remote_copy(
            ptot, ptr.at[x], ps.at[d], pr.at[d], device_id=(to, head), device_id_type=MESH
        )

    pl.semaphore_wait(barrier, (nz - 1) + (nx - 1) + 3)
    halo_copy(1).start()
    halo_copy(0).start()

    @pl.loop(1, nz)
    def _(d):
        pas_copy(d).start()

    @pl.loop(0, chans // LANES)
    def _(i):
        cols = pl.ds(pl.multiple_of(i * LANES, LANES), LANES)
        xf[pl.ds(8, tok), cols] = xin[:, cols].astype(F32)
        acc = jnp.broadcast_to(bias[:, cols], (tok, LANES))
        for lag in range(4):
            term = taps[3 - lag : 4 - lag, cols] * xf[pl.ds(8 - lag, tok), cols]
            acc = acc + (term if lag == 0 else jnp.where(offb[...] >= lag, term, 0.0))
        xc[:, cols] = silu(acc).astype(BF16)

    xfb[pl.ds(8, tok), :] = bcin[...].astype(F32)
    halo_copy(1).wait()
    xfb[pl.ds(0, 8), :] = bchalo[...].astype(F32)[8:16]
    for i in range(state // LANES):
        cols = slice(i * LANES, (i + 1) * LANES)
        acc = jnp.broadcast_to(bcb[:, cols], (tok, LANES))
        for lag in range(4):
            term = bct[3 - lag : 4 - lag, cols] * xfb[pl.ds(8 - lag, tok), cols]
            acc = acc + (term if lag == 0 else jnp.where(offb[...] >= lag, term, 0.0))
        bown[:, cols] = silu(acc).astype(BF16)
    partner_copy().start()

    halo_copy(0).wait()
    xf[pl.ds(0, 8), :] = xhalo[...].astype(F32)[8:16]
    acc = jnp.broadcast_to(bias[...], (16, chans))
    off_top = offb[0:16, 0:1]
    for lag in range(4):
        term = taps[3 - lag : 4 - lag, :] * xf[pl.ds(8 - lag, 16), :]
        acc = acc + (term if lag == 0 else jnp.where(off_top >= lag, term, 0.0))
    xc[0:16, :] = silu(acc).astype(BF16)

    partner_copy().wait()
    even = lax.rem(head, 2) == 0
    bsel[...] = jnp.where(even, bown[...], bother[...])
    csel[...] = jnp.where(even, bother[...], bown[...])

    for c in range(nc):
        cols = slice(c * width, (c + 1) * width)
        scaled = (xc[:, cols].astype(F32) * sexp[:, cols]).astype(BF16)
        block_state = lax.dot_general(bsel[...], scaled, (((0,), (0,)), ((), ())), preferred_element_type=F32)
        st[c] = block_state.astype(BF16).reshape(nz, rows, width)
        recv[c, pl.ds(z, 1)] = st[c, pl.ds(z, 1)]

        @pl.loop(1, nz)
        def _(d):
            fwd_copy(c, d).start()

    scores = lax.dot_general(csel[...], bsel[...], (((1,), (1,)), ((), ())), preferred_element_type=F32)
    row_i, col_j = iota((tok, tok), 0).astype(F32), iota((tok, tok), 1).astype(F32)
    linked = (col_j <= row_i) & (offb[:, 0:1] >= row_i - col_j)
    smask[...] = jnp.where(linked, scores, 0.0)
    spread_f = iota((heads, chans), 0) == iota((heads, chans), 1) // HEADDIM
    skip = jnp.sum(jnp.where(spread_f, jnp.broadcast_to(column(sgain[...]), (heads, chans)), 0.0), axis=0, keepdims=True)
    y[...] = skip * xc[...].astype(F32)
    first = iota((tok, LANES), 1) < HEADDIM

    @pl.loop(0, heads // 2)
    def _(p):
        cols = pl.ds(pl.multiple_of(p * LANES, LANES), LANES)
        rate_cols = rexp[:, cols]
        xp = xc[:, cols]
        parts = []
        for k in range(2):
            gap = jnp.minimum(rate_cols[:, k * HEADDIM : k * HEADDIM + 1] - rate[pl.ds(2 * p + k, 1), :], 0.0)
            weights = (smask[...] * jnp.exp(gap) * td[pl.ds(2 * p + k, 1), :]).astype(BF16)
            parts.append(jnp.dot(weights, xp, preferred_element_type=F32))
        y[:, cols] = y[:, cols] + jnp.where(first, parts[0], parts[1])

    @pl.loop(1, nz)
    def _(d):
        pas_copy(d).wait()

    spread_l = (iota((LANES, chans), 0) == iota((LANES, chans), 1) // HEADDIM).astype(BF16)

    def expand_rows(value):
        return sum(jnp.dot(part, spread_l, preferred_element_type=F32) for part in split3(value))

    pas_all = pas_r[:, 0, :]
    pexp[...] = expand_rows(pas_all)
    product = pas_all[0:1]
    for k in range(1, nz):
        product = product * pas_all[k : k + 1]
    ptot[...] = jnp.broadcast_to(product, (8, LANES))

    @pl.loop(1, nx)
    def _(d):
        ptot_copy(d).start()

    def advance(c, k, carried):
        cols = slice(c * width, (c + 1) * width)
        return pexp[pl.ds(k, 1), cols] * carried + recv[c, k].astype(F32)

    def totals(c):
        @pl.loop(1, nz)
        def _(d):
            fwd_copy(c, d).wait()

        total = lax.fori_loop(0, nz, lambda k, e: advance(c, k, e), jnp.zeros((rows, width), F32))
        tb[c] = total.astype(BF16)

        @pl.loop(1, nx)
        def _(d):
            total_copy(c, d).start()

    def give_back(c):
        if c == 0:

            @pl.loop(1, nx)
            def _(d):
                ptot_copy(d).wait()

        @pl.loop(1, nx)
        def _(d):
            total_copy(c, d).wait()

        cols = slice(c * width, (c + 1) * width)
        carried = jnp.zeros((rows, width), F32)
        for k in range(nx - 1):
            decay = expand_rows(ptr[k])[0:1, cols]
            longer = decay * carried + tr[c, k].astype(F32)
            carried = jnp.where(k < x, longer, carried)

        def pass_on(k, e):
            eb[c, k] = e.astype(BF16)
            return advance(c, k, e)

        lax.fori_loop(0, nz, pass_on, carried)
        ent[c, pl.ds(z, 1)] = eb[c, pl.ds(z, 1)]

        @pl.loop(1, nz)
        def _(d):
            ret_copy(c, d).start()

    def finish(c):
        @pl.loop(1, nz)
        def _(d):
            ret_copy(c, d).wait()

        cols = slice(c * width, (c + 1) * width)
        read = jnp.dot(csel[...], ent[c].reshape(state, width), preferred_element_type=F32)
        carries = offb[:, 0:1] >= iota((tok, 1), 0).astype(F32) + 1.0
        scale = jnp.where(carries, jnp.exp(rexp[:, cols]), 0.0)
        out[:, cols] = (y[:, cols] + read * scale).astype(BF16)

    for c in range(nc):
        totals(c)
        if c:
            give_back(c - 1)
    give_back(nc - 1)
    for c in range(nc):
        finish(c)


def on_device(nx, nz, nc, *args):
    (ssm_input, bc_input, conv_taps, conv_bias, bc_taps, bc_bias, step_input, step_bias, decay_log, skip_gain,
     request_offset) = args
    tok, chans = ssm_input.shape
    state = bc_input.shape[1]
    heads = step_input.shape[0]
    width, rows = chans // nc, state // nz
    vmem = pl.BlockSpec(memory_space=pltpu.VMEM)
    dma = pltpu.SemaphoreType.DMA
    scratch = [
        pltpu.VMEM((tok + 8, chans), F32),
        pltpu.VMEM((tok + 8, state), F32),
        pltpu.VMEM((tok, chans), BF16),
        pltpu.VMEM((tok, LANES), F32),
        pltpu.VMEM((tok, chans), F32),
        pltpu.VMEM((tok, chans), F32),
        pltpu.VMEM((heads, tok), F32),
        pltpu.VMEM((heads, tok), F32),
        pltpu.VMEM((16, chans), BF16),
        pltpu.VMEM((16, state), BF16),
        pltpu.VMEM((tok, state), BF16),
        pltpu.VMEM((tok, state), BF16),
        pltpu.VMEM((tok, state), BF16),
        pltpu.VMEM((tok, state), BF16),
        pltpu.VMEM((tok, tok), F32),
        pltpu.VMEM((tok, chans), F32),
        pltpu.VMEM((nc, nz, rows, width), BF16),
        pltpu.VMEM((nc, nz, rows, width), BF16),
        pltpu.VMEM((nc, nz, rows, width), BF16),
        pltpu.VMEM((nc, nz, rows, width), BF16),
        pltpu.VMEM((8, LANES), F32),
        pltpu.VMEM((nz, 8, LANES), F32),
        pltpu.VMEM((nz, chans), F32),
        pltpu.VMEM((nc, rows, width), BF16),
        pltpu.VMEM((nc, nx, rows, width), BF16),
        pltpu.VMEM((8, LANES), F32),
        pltpu.VMEM((nx, 8, LANES), F32),
        dma((nc, nz)), dma((nc, nz)), dma((nc, nz)), dma((nc, nz)),
        dma((nc, nx)), dma((nc, nx)), dma((nx,)), dma((nx,)), dma((nz,)), dma((nz,)), dma((3,)), dma((3,)),
    ]
    return pl.pallas_call(
        functools.partial(kernel, nx, nz, nc),
        out_shape=jax.ShapeDtypeStruct((tok, chans), BF16),
        in_specs=[vmem] * 11,
        out_specs=vmem,
        scratch_shapes=scratch,
        compiler_params=pltpu.CompilerParams(
            collective_id=0, has_side_effects=True, vmem_limit_bytes=40 << 20
        ),
    )(
        ssm_input, bc_input, conv_taps, conv_bias[None], bc_taps, bc_bias[None], step_input, step_bias[None],
        decay_log[None], skip_gain[None], request_offset[None],
    )


def solution(mesh, nx=4, nc=2):
    nz = mesh.shape["seq"] // nx
    return jax.shard_map(
        functools.partial(on_device, nx, nz, nc),
        mesh=mesh,
        in_specs=(
            P("seq", "head"),
            P("seq", "head"),
            P(None, "head"),
            P("head"),
            P(None, "head"),
            P("head"),
            P("head", "seq"),
            P("head"),
            P("head"),
            P("head"),
            P("seq"),
        ),
        out_specs=P("seq", "head"),
        check_vma=False,
    )
```

time: 897 us -> 85.5 us (0.10)
  waiting for transfers between devices: 396 us -> 0 us
  other arithmetic: 213 us -> 0 us
  local copies, waits for them, and re-layouts: 131 us -> 5.56 us
  blocking collectives: 118 us -> 0 us
  Pallas kernels: 0 us -> 79.6 us
  between operations: 14.9 us -> 0.05 us
  starting transfers between devices: 11.3 us -> 0 us
    all_gather x1 -> x0, waiting for transfers between devices: 396 us -> none  [prefix(): pieces = jax.tree.map(lambda part: lax.all_gather(part, axis), value)]
    select_n x63 -> x0, other arithmetic: 205 us -> none  [hop(): jnp.where(position < mine, new, old)]
    dynamic_slice x126 -> x0, local copies, waits for them, and re-layouts: 121 us -> none  [hop(): longer = join(total, jax.tree.map(lambda part: part[position], pieces))]
    unnamed x1 -> x0, blocking collectives: 118 us -> none
    pallas_call x0 -> x1, Pallas kernels: none -> 79.6 us  [on_device(): pl.pallas_call(functools.partial(kernel, nx, nz, nc), out_shape=jax.Shape...]
    ppermute x3 -> x0, starting transfers between devices: 11.3 us -> none  [the longest x2 7.89 us: passed_along(): return lax.ppermute(block, axis, route)]
  transfers between devices with their start and end apart: 4 -> 0, of which waited for: 1 -> 0; matrix products, arithmetic and copies ran while one was open for 2% -> 0% of each run, Pallas kernels for 0% -> 0%
where the time goes in v1:
time: 85.5 us; the launch traced here: 85.2 us
  Pallas kernels  79.6 us (93%)
  local copies, waits for them, and re-layouts  5.56 us (7%)
    pallas_call x1, Pallas kernels, on_device(): pl.pallas_call(functools.partial(kernel, nx, nz, nc), out_shape=jax.Shape...  79.6 us
    unnamed x23, local copies, waits for them, and re-layouts  5.56 us

profile of v1, /device:TPU:1, one launch (start us, length us, event | category | flops | bytes accessed | tf_op | source)
XLA Modules:
  0.0 85.2 jit_solution(8145411771559855070)
XLA Ops:
  0.0 0.0 copy-start.7
  0.0 0.0 copy-start.8
  0.0 0.0 copy-start.9
  0.0 0.0 copy-start.5
  0.0 0.0 copy-start.4
  0.0 0.0 copy-start.6
  0.0 0.6 copy-done.7
  0.7 0.0 copy-done.8
  0.7 0.0 copy-done.9
  0.7 0.0 copy-done.5
  0.7 0.0 copy-done.4
  0.8 0.0 copy-done.6
  0.8 0.0 copy-start
  0.8 1.0 %copy-done = bf16[256,1024]{1,0:T(8,128)(2,1)S(1)} copy-done((bf16[256,1024]{1,0:T(8,128)(2,1)S(1)}, bf16[256,1024]{1,0:T(8,128)(2,1)}, u32[]{:S(2)}) %copy-start) | copy-done | bytes 524312
  1.8 0.0 copy-start.1
  1.8 0.9 %copy-done.1 = bf16[256,256]{1,0:T(8,128)(2,1)S(1)} copy-done((bf16[256,256]{1,0:T(8,128)(2,1)S(1)}, bf16[256,256]{1,0:T(8,128)(2,1)}, u32[]{:S(2)}) %copy-start.1) | copy-done | bytes 131096
  2.7 0.0 copy-start.2
  2.7 0.7 copy-done.2
  3.4 0.0 copy-start.3
  3.4 0.7 copy-done.3
  4.1 0.0 copy-start.10
  4.1 0.7 copy-done.10
  4.8 79.6 %shard_map.109 = bf16[256,1024]{1,0:T(8,128)(2,1)S(1)} custom-call(bf16[256,1024]{1,0:T(8,128)(2,1)S(1)} %copy-done, bf16[256,256]{1,0:T(8,128)(2,1)S(1)} %copy-done.1, f32[4,1024]{1,0:T(4,128)S(1)} %copy-done.2, f32[1,1024]{1,0:T(1,128)S(1)} %bitcast.6, f32[4,256]{1,0:T(4,128)S(1)} %copy-done.5, f32[1,256]{1,0:T(1,128)S(1)} %bitcast.7, ...), custom_call_target="tpu_custom_call" | custom-call | tf_op jit(solution)/shard_map/pallas_call | solution.py:359
  84.4 0.8 copy.13
Async XLA Ops:
  0.0 0.7 copy-start.7
  0.0 0.7 copy-start.8
  0.0 0.7 copy-start.9
  0.0 0.7 copy-start.5
  0.0 0.7 copy-start.4
  0.0 0.7 copy-start.6
  0.8 1.0 %copy-start = (bf16[256,1024]{1,0:T(8,128)(2,1)S(1)}, bf16[256,1024]{1,0:T(8,128)(2,1)}, u32[]{:S(2)}) copy-start(bf16[256,1024]{1,0:T(8,128)(2,1)} %xin.1) | copy-start | bytes 1572868
  1.8 0.9 %copy-start.1 = (bf16[256,256]{1,0:T(8,128)(2,1)S(1)}, bf16[256,256]{1,0:T(8,128)(2,1)}, u32[]{:S(2)}) copy-start(bf16[256,256]{1,0:T(8,128)(2,1)} %bcin.1) | copy-start | bytes 393220
  2.7 0.7 copy-start.2
  3.4 0.7 copy-start.3
  4.1 0.7 copy-start.10

commit v2 on v1

v2 whole, which is shorter than its diff:
```python
import functools

import jax
import jax.numpy as jnp
from jax import lax
from jax.experimental import pallas as pl
from jax.experimental.pallas import tpu as pltpu
from jax.sharding import PartitionSpec as P

HEADDIM = 64
LANES = 128
MESH = pl.DeviceIdType.MESH
F32 = jnp.float32
BF16 = jnp.bfloat16


def split3(value):
    high = value.astype(BF16)
    rest = value - high.astype(F32)
    mid = rest.astype(BF16)
    low = (rest - mid.astype(F32)).astype(BF16)
    return high, mid, low


def iota(shape, axis):
    return lax.broadcasted_iota(jnp.int32, shape, axis)


def silu(v):
    return v / (1.0 + jnp.exp(-v))


def kernel(
    nx, ni, nr, nc,
    xin, bcin_h, taps_h, bias_h, bct_h, bcb_h, step_h, sbias_h, dlog_h, sgain_h, off_h,
    out,
    xv, bcin, taps, bias, bct, bcb, step, sbias, dlog, sgain, off,
    xf, xfb, xc, offb, sexp, xs, rexp, rate, td, skip, xhalo, bchalo, bown, bother, bsel, csel,
    smask, y, st, ra, gs, rb, kb, kr, eb, ent, pas_s, pas_r, gpas_s, gpas_r, pexp, gexp,
    ins, a_s, a_r, b_s, b_r, k_s, k_r, e_s, e_r, q_s, q_r, p_s, p_r, h_s, h_r, round_sem,
):
    tok, chans = xv.shape
    state = bcin.shape[1]
    heads = step.shape[0]
    width = chans // nc
    count = lax.axis_size("seq")
    nq = count // ni
    nb = nq // nr
    ng = nq // nx
    rows_a, rows_b, part_width = state // ni, state // ni // nr, width // nb
    s = lax.axis_index("seq")
    head = lax.axis_index("head")
    odd = lax.rem(head, 2)
    partner = head + 1 - 2 * odd
    nxt = lax.rem(s + 1, count)
    prv = lax.rem(s + count - 1, count)
    shift = odd * (ni // 2)
    place = lax.rem(s + shift, count)
    q, i = place // ni, lax.rem(place, ni)

    def device(q_at, i_at):
        return (lax.rem(q_at * ni + i_at + count - shift, count), head)

    def member(d):
        return lax.rem(i + d, ni)

    def group(d):
        return lax.rem(q + d, nq)

    loads = [
        pltpu.make_async_copy(src, dst, ins.at[k])
        for k, (src, dst) in enumerate(
            (
                (off_h, off), (step_h, step), (sbias_h, sbias), (dlog_h, dlog), (bcin_h, bcin), (xin, xv),
                (taps_h, taps), (bias_h, bias), (bct_h, bct), (bcb_h, bcb), (sgain_h, sgain),
            )
        )
    ]
    for load in loads:
        load.start()

    barrier = pltpu.get_barrier_semaphore()

    def greet(device_id):
        pl.semaphore_signal(barrier, inc=1, device_id=device_id, device_id_type=MESH)

    def beside(d):
        return device(q // ng * ng + lax.rem(lax.rem(q, ng) + d, ng), i)

    greet(beside(1))
    greet(beside(ng - 1))

    @pl.loop(1, ni)
    def _(d):
        greet(device(q, member(d)))

    @pl.loop(1, nx)
    def _(d):
        greet(device(group(d * ng), i))

    greet((nxt, head))
    greet((prv, head))
    greet((s, partner))

    def tell(r):
        for d in (1, ng - 1):
            pl.semaphore_signal(round_sem.at[r], inc=1, device_id=beside(d), device_id_type=MESH)

    def remote(src, dst, send, recv, device_id):
        return pltpu.make_async_remote_copy(src, dst, send, recv, device_id=device_id, device_id_type=MESH)

    def halo_copy(which):
        src = (xin, bcin_h)[which].at[pl.ds(tok - 16, 16), :]
        return remote(src, (xhalo, bchalo)[which], h_s.at[which], h_r.at[which], (nxt, head))

    def partner_copy():
        return remote(bown, bother, h_s.at[2], h_r.at[2], (s, partner))

    def pas_copy(d):
        return remote(pas_s, pas_r.at[i], q_s.at[d], q_r.at[d], device(q, member(d)))

    def gpas_copy(d):
        return remote(gpas_s, gpas_r.at[q], p_s.at[d], p_r.at[d], device(group(d), i))

    def a_copy(c, d):
        to = member(d)
        return remote(st.at[c, to], ra.at[c, i], a_s.at[c, d], a_r.at[c, d], device(q, to))

    def b_copy(c, d):
        to = group(d)
        return remote(gs.at[c, to], rb.at[c, q], b_s.at[c, d], b_r.at[c, d], device(to, i))

    def k_copy(c, d):
        to = group(d)
        return remote(kb.at[c, to], kr.at[c, q], k_s.at[c, d], k_r.at[c, d], device(to, i))

    def e_copy(c, d):
        to = member(d)
        return remote(eb.at[c, to], ent.at[c, i], e_s.at[c, d], e_r.at[c, d], device(q, to))

    def start(copy, n, *lead):
        @pl.loop(1, n)
        def _(d):
            copy(*lead, d).start()

    def wait(copy, n, *lead):
        @pl.loop(1, n)
        def _(d):
            copy(*lead, d).wait()

    for load in loads[:4]:
        load.wait()
    off_row = jnp.minimum(off[...], tok).astype(F32)
    eye = (iota((tok, tok), 0) == iota((tok, tok), 1)).astype(BF16)
    off_rows = jnp.broadcast_to(off_row, (LANES, tok)).astype(BF16)
    offb[...] = lax.dot_general(eye, off_rows, (((1,), (1,)), ((), ())), preferred_element_type=F32)
    off_last = off_row[:, tok - 1 : tok]

    eye_h = iota((heads, heads), 0) == iota((heads, heads), 1)

    def column(row):
        return jnp.sum(jnp.where(eye_h, jnp.broadcast_to(row, (heads, heads)), 0.0), axis=1, keepdims=True)

    time_step = jnp.log1p(jnp.exp(step[...] + column(sbias[...])))
    log_decay = -jnp.exp(column(dlog[...])) * time_step
    upper = (iota((tok, tok), 0) <= iota((tok, tok), 1)).astype(F32)
    rate_row = jnp.dot(log_decay, upper, precision=lax.Precision.HIGHEST, preferred_element_type=F32)
    rate[...] = rate_row
    td[...] = time_step
    rate_last = rate_row[:, tok - 1 : tok]
    position = iota((1, tok), 1).astype(F32)
    tail = off_last >= (tok - 1) - position
    s_row = jnp.where(tail, jnp.exp(rate_last - rate_row), 0.0) * time_step
    passing = jnp.where(off_last >= tok, jnp.exp(rate_last), 0.0)

    pick = iota((heads, LANES), 0) == iota((heads, LANES), 1)
    as_row = jnp.sum(jnp.where(pick, jnp.broadcast_to(passing, (heads, LANES)), 0.0), axis=0, keepdims=True)
    pas_s[...] = jnp.broadcast_to(as_row, (8, LANES))

    spread = (lax.rem(iota((3 * heads, chans), 0), heads) == iota((3 * heads, chans), 1) // HEADDIM).astype(BF16)

    def expand(value):
        return lax.dot_general(
            jnp.concatenate(split3(value), axis=0), spread, (((0,), (0,)), ((), ())), preferred_element_type=F32
        )

    sexp[...] = expand(s_row)
    rexp[...] = expand(rate_row)

    for load in loads[5:8]:
        load.wait()

    @pl.loop(0, chans // LANES)
    def _(n):
        cols = pl.ds(pl.multiple_of(n * LANES, LANES), LANES)
        xf[pl.ds(8, tok), cols] = xv[:, cols].astype(F32)
        acc = jnp.broadcast_to(bias[:, cols], (tok, LANES))
        for lag in range(4):
            term = taps[3 - lag : 4 - lag, cols] * xf[pl.ds(8 - lag, tok), cols]
            acc = acc + (term if lag == 0 else jnp.where(offb[...] >= lag, term, 0.0))
        xc[:, cols] = silu(acc).astype(BF16)

    pl.semaphore_wait(barrier, (ni - 1) + (nx - 1) + 5)
    halo_copy(1).start()
    halo_copy(0).start()
    tell(0)
    pas_r[pl.ds(i, 1)] = pas_s[...][None]
    start(pas_copy, ni)

    @pl.loop(0, chans // LANES)
    def _(n):
        cols = pl.ds(pl.multiple_of(n * LANES, LANES), LANES)
        xs[:, cols] = (xc[:, cols].astype(F32) * sexp[:, cols]).astype(BF16)

    loads[4].wait()
    loads[8].wait()
    loads[9].wait()
    xfb[pl.ds(8, tok), :] = bcin[...].astype(F32)
    halo_copy(1).wait()
    xfb[pl.ds(0, 8), :] = bchalo[...].astype(F32)[8:16]
    for n in range(state // LANES):
        cols = slice(n * LANES, (n + 1) * LANES)
        acc = jnp.broadcast_to(bcb[:, cols], (tok, LANES))
        for lag in range(4):
            term = bct[3 - lag : 4 - lag, cols] * xfb[pl.ds(8 - lag, tok), cols]
            acc = acc + (term if lag == 0 else jnp.where(offb[...] >= lag, term, 0.0))
        bown[:, cols] = silu(acc).astype(BF16)
    partner_copy().start()

    halo_copy(0).wait()
    xf[pl.ds(0, 8), :] = xhalo[...].astype(F32)[8:16]
    acc = jnp.broadcast_to(bias[...], (16, chans))
    off_top = offb[0:16, 0:1]
    for lag in range(4):
        term = taps[3 - lag : 4 - lag, :] * xf[pl.ds(8 - lag, 16), :]
        acc = acc + (term if lag == 0 else jnp.where(off_top >= lag, term, 0.0))
    top = silu(acc).astype(BF16)
    xc[0:16, :] = top
    xs[0:16, :] = (top.astype(F32) * sexp[0:16, :]).astype(BF16)

    partner_copy().wait()
    even = odd == 0
    bsel[...] = jnp.where(even, bown[...], bother[...])
    csel[...] = jnp.where(even, bother[...], bown[...])

    for c in range(nc):
        cols = slice(c * width, (c + 1) * width)
        block_state = lax.dot_general(bsel[...], xs[:, cols], (((0,), (0,)), ((), ())), preferred_element_type=F32)
        st[c] = block_state.astype(BF16).reshape(ni, rows_a, width)
        start(a_copy, ni, c)
        ra[c, pl.ds(i, 1)] = st[c, pl.ds(i, 1)]

    pl.semaphore_wait(round_sem.at[0], 2)
    tell(1)

    wait(pas_copy, ni)
    pas_all = pas_r[:, 0, :]
    product = pas_all[0:1]
    for m in range(1, ni):
        product = product * pas_all[m : m + 1]
    gpas_s[...] = jnp.broadcast_to(product, (8, LANES))
    gpas_r[pl.ds(q, 1)] = gpas_s[...][None]

    spread_l = (iota((LANES, chans), 0) == iota((LANES, chans), 1) // HEADDIM).astype(BF16)

    def expand_rows(value):
        return sum(jnp.dot(part, spread_l, preferred_element_type=F32) for part in split3(value))

    pexp[...] = expand_rows(pas_all)

    loads[10].wait()
    scores = lax.dot_general(csel[...], bsel[...], (((1,), (1,)), ((), ())), preferred_element_type=F32)
    row_i, col_j = iota((tok, tok), 0).astype(F32), iota((tok, tok), 1).astype(F32)
    linked = (col_j <= row_i) & (offb[:, 0:1] >= row_i - col_j)
    smask[...] = jnp.where(linked, scores, 0.0)
    spread_f = iota((heads, chans), 0) == iota((heads, chans), 1) // HEADDIM
    skip[...] = jnp.sum(jnp.where(spread_f, jnp.broadcast_to(column(sgain[...]), (heads, chans)), 0.0), axis=0, keepdims=True)
    first = iota((tok, LANES), 1) < HEADDIM
    carries = offb[...] >= iota((tok, LANES), 0).astype(F32) + 1.0

    @pl.loop(0, heads // 2)
    def _(p):
        cols = pl.ds(pl.multiple_of(p * LANES, LANES), LANES)
        rate_cols = rexp[:, cols]
        xp = xc[:, cols]
        parts = []
        for k in range(2):
            gap = jnp.minimum(rate_cols[:, k * HEADDIM : k * HEADDIM + 1] - rate[pl.ds(2 * p + k, 1), :], 0.0)
            weights = (smask[...] * jnp.exp(gap) * td[pl.ds(2 * p + k, 1), :]).astype(BF16)
            parts.append(jnp.dot(weights, xp, preferred_element_type=F32))
        rexp[:, cols] = jnp.where(carries, jnp.exp(rate_cols), 0.0)
        y[:, cols] = skip[:, cols] * xp.astype(F32) + jnp.where(first, parts[0], parts[1])

    def in_group(c, m, carried, cols):
        carried = jnp.where((q == 0) & (m == shift), 0.0, carried)
        later = pexp[pl.ds(m, 1), c * width + cols.start : c * width + cols.stop] * carried
        return carried, later + ra[c, m, :, cols].astype(F32)

    def part(b):
        return slice(b * part_width, (b + 1) * part_width)

    def group_total(c):
        if c == 0:
            pl.semaphore_wait(round_sem.at[1], 2)
            start(gpas_copy, nq)
        wait(a_copy, ni, c)
        for b in range(nb):
            total = jnp.zeros((rows_a, part_width), F32)
            for m in range(ni):
                total = in_group(c, m, total, part(b))[1]
            gs[c, b * nr : (b + 1) * nr] = total.astype(BF16).reshape(nr, rows_b, part_width)
        start(b_copy, nq, c)
        rb[c, pl.ds(q, 1)] = gs[c, pl.ds(q, 1)]

    def over_groups(c):
        if c == 0:
            wait(gpas_copy, nq)
            every = expand_rows(gpas_r[:, 0, :])
            for n in range(nc):
                for b in range(nb):

                    @pl.when(q // nr == b)
                    def _():
                        gexp[n] = every[:, n * width + b * part_width : n * width + (b + 1) * part_width]

        wait(b_copy, nq, c)

        def pass_on(k, carried):
            kb[c, k] = carried.astype(BF16)
            return gexp[c, pl.ds(k, 1), :] * carried + rb[c, k].astype(F32)

        kb[c, 0] = lax.fori_loop(0, nq, pass_on, jnp.zeros((rows_b, part_width), F32)).astype(BF16)
        start(k_copy, nq, c)
        kr[c, pl.ds(q, 1)] = kb[c, pl.ds(q, 1)]

    def to_devices(c):
        wait(k_copy, nq, c)
        for b in range(nb):
            carried = kr[c, b * nr : (b + 1) * nr].astype(F32).reshape(rows_a, part_width)
            for m in range(ni):
                entering, carried = in_group(c, m, carried, part(b))
                eb[c, m, :, part(b)] = entering.astype(BF16)
        start(e_copy, ni, c)
        ent[c, pl.ds(i, 1)] = eb[c, pl.ds(i, 1)]

    def finish(c):
        wait(e_copy, ni, c)
        cols = slice(c * width, (c + 1) * width)
        read = jnp.dot(csel[...], ent[c].reshape(state, width), preferred_element_type=F32)
        out[:, cols] = (y[:, cols] + read * rexp[:, cols]).astype(BF16)

    for stage in (group_total, over_groups, to_devices, finish):
        for c in range(nc):
            stage(c)


def on_device(nx, ni, nr, nc, *args):
    (ssm_input, bc_input, conv_taps, conv_bias, bc_taps, bc_bias, step_input, step_bias, decay_log, skip_gain,
     request_offset) = args
    tok, chans = ssm_input.shape
    state = bc_input.shape[1]
    heads = step_input.shape[0]
    nq = lax.axis_size("seq") // ni
    width, rows_a = chans // nc, state // ni
    rows_b, part_width = rows_a // nr, width // (nq // nr)
    anywhere = pl.BlockSpec(memory_space=pl.ANY)
    operands = (
        ssm_input, bc_input, conv_taps, conv_bias[None], bc_taps, bc_bias[None], step_input, step_bias[None],
        decay_log[None], skip_gain[None], request_offset[None],
    )
    vmem, dma = pltpu.VMEM, pltpu.SemaphoreType.DMA
    scratch = [
        *[vmem(a.shape, a.dtype) for a in operands],
        vmem((tok + 8, chans), F32),
        vmem((tok + 8, state), F32),
        vmem((tok, chans), BF16),
        vmem((tok, LANES), F32),
        vmem((tok, chans), F32),
        vmem((tok, chans), BF16),
        vmem((tok, chans), F32),
        vmem((heads, tok), F32),
        vmem((heads, tok), F32),
        vmem((1, chans), F32),
        vmem((16, chans), BF16),
        vmem((16, state), BF16),
        vmem((tok, state), BF16),
        vmem((tok, state), BF16),
        vmem((tok, state), BF16),
        vmem((tok, state), BF16),
        vmem((tok, tok), F32),
        vmem((tok, chans), F32),
        vmem((nc, ni, rows_a, width), BF16),
        vmem((nc, ni, rows_a, width), BF16),
        vmem((nc, nq, rows_b, part_width), BF16),
        vmem((nc, nq, rows_b, part_width), BF16),
        vmem((nc, nq, rows_b, part_width), BF16),
        vmem((nc, nq, rows_b, part_width), BF16),
        vmem((nc, ni, rows_a, width), BF16),
        vmem((nc, ni, rows_a, width), BF16),
        vmem((8, LANES), F32),
        vmem((8, 8, LANES), F32),
        vmem((8, LANES), F32),
        vmem((nq, 8, LANES), F32),
        vmem((8, chans), F32),
        vmem((nc, nq, part_width), F32),
        dma((len(operands),)),
        *[dma((nc, n)) for n in (ni, nq, nq, ni) for _ in range(2)],
        *[dma((n,)) for n in (ni, nq, 3) for _ in range(2)],
        pltpu.SemaphoreType.REGULAR((2,)),
    ]
    return pl.pallas_call(
        functools.partial(kernel, nx, ni, nr, nc),
        out_shape=jax.ShapeDtypeStruct((tok, chans), BF16),
        in_specs=[anywhere] * len(operands),
        out_specs=pl.BlockSpec(memory_space=pltpu.VMEM),
        scratch_shapes=scratch,
        compiler_params=pltpu.CompilerParams(
            collective_id=0, has_side_effects=True, vmem_limit_bytes=56 << 20
        ),
    )(*operands)


def solution(mesh, nx=4, ni=4, nr=4, nc=2):
    return jax.shard_map(
        functools.partial(on_device, nx, ni, nr, nc),
        mesh=mesh,
        in_specs=(
            P("seq", "head"),
            P("seq", "head"),
            P(None, "head"),
            P("head"),
            P(None, "head"),
            P("head"),
            P("head", "seq"),
            P("head"),
            P("head"),
            P("head"),
            P("seq"),
        ),
        out_specs=P("seq", "head"),
        check_vma=False,
    )
```

time: 85.5 us -> 64.8 us (0.76)
  the two profiles are of different devices: /device:TPU:1 before, /device:TPU:8 now
where the time goes in v2:
time: 64.8 us; the launch traced here: 64.7 us
  Pallas kernels  62.8 us (97%)
  local copies, waits for them, and re-layouts  1.87 us (3%)
    pallas_call x1, Pallas kernels, on_device(): pl.pallas_call(functools.partial(kernel, nx, ni, nr, nc), out_shape=jax.S...  62.8 us
    unnamed x1, local copies, waits for them, and re-layouts  1.87 us

profile of v2, /device:TPU:8, one launch (start us, length us, event | category | flops | bytes accessed | tf_op | source)
XLA Modules:
  0.0 64.7 jit_solution(4436914078541938305)
XLA Ops:
  0.0 62.8 %shard_map.109 = bf16[256,1024]{1,0:T(8,128)(2,1)} custom-call(bf16[256,1024]{1,0:T(8,128)(2,1)} %xin.1, bf16[256,256]{1,0:T(8,128)(2,1)} %bcin_h.1, f32[4,1024]{1,0:T(4,128)} %taps_h.1, f32[1,1024]{1,0:T(1,128)} %bitcast.6, f32[4,256]{1,0:T(4,128)} %bct_h.1, f32[1,256]{1,0:T(1,128)} %bitcast.7, f32[16,256]{1,0:T(8,128)} %step_h.1, f32[1,16]{1,0:T(1,128)} %bitcast.9, ...), custom_call_target="tpu_custom_call" | custom-call | tf_op jit(solution)/shard_map/pallas_call | solution.py:411
  62.8 1.9 %copy.13 = bf16[256,1024]{1,0:T(8,128)(2,1)} copy(bf16[256,1024]{1,0:T(8,128)(2,1)} %shard_map.109) | data formatting | bytes 1048576

commit v3 on v2

--- a/solution.py
+++ b/solution.py
@@ -54,7 +54,7 @@
     partner = head + 1 - 2 * odd
     nxt = lax.rem(s + 1, count)
     prv = lax.rem(s + count - 1, count)
-    shift = odd * (ni // 2)
+    shift = (1 - odd) * (ni // 2)
     place = lax.rem(s + shift, count)
     q, i = place // ni, lax.rem(place, ni)
 
@@ -117,36 +117,33 @@
         return remote(bown, bother, h_s.at[2], h_r.at[2], (s, partner))
 
     def pas_copy(d):
-        return remote(pas_s, pas_r.at[i], q_s.at[d], q_r.at[d], device(q, member(d)))
+        return remote(pas_s, pas_r.at[i], q_s.at[0], q_r.at[0], device(q, member(d)))
 
     def gpas_copy(d):
-        return remote(gpas_s, gpas_r.at[q], p_s.at[d], p_r.at[d], device(group(d), i))
+        return remote(gpas_s, gpas_r.at[q], p_s.at[0], p_r.at[0], device(group(d), i))
 
     def a_copy(c, d):
         to = member(d)
-        return remote(st.at[c, to], ra.at[c, i], a_s.at[c, d], a_r.at[c, d], device(q, to))
+        return remote(st.at[c, to], ra.at[c, i], a_s.at[c], a_r.at[c], device(q, to))
 
     def b_copy(c, d):
         to = group(d)
-        return remote(gs.at[c, to], rb.at[c, q], b_s.at[c, d], b_r.at[c, d], device(to, i))
+        return remote(gs.at[c, to], rb.at[c, q], b_s.at[c], b_r.at[c], device(to, i))
 
     def k_copy(c, d):
         to = group(d)
-        return remote(kb.at[c, to], kr.at[c, q], k_s.at[c, d], k_r.at[c, d], device(to, i))
+        return remote(kb.at[c, to], kr.at[c, q], k_s.at[c], k_r.at[c], device(to, i))
 
     def e_copy(c, d):
         to = member(d)
-        return remote(eb.at[c, to], ent.at[c, i], e_s.at[c, d], e_r.at[c, d], device(q, to))
+        return remote(eb.at[c, to], ent.at[c, i], e_s.at[c], e_r.at[c], device(q, to))
 
     def start(copy, n, *lead):
-        @pl.loop(1, n)
-        def _(d):
+        for d in range(1, n):
             copy(*lead, d).start()
 
-    def wait(copy, n, *lead):
-        @pl.loop(1, n)
-        def _(d):
-            copy(*lead, d).wait()
+    def arrived(ref, sem):
+        pltpu.make_async_copy(ref, ref, sem).wait()
 
     for load in loads[:4]:
         load.wait()
@@ -253,7 +250,7 @@
     pl.semaphore_wait(round_sem.at[0], 2)
     tell(1)
 
-    wait(pas_copy, ni)
+    arrived(pas_r.at[pl.ds(0, ni - 1)], q_r.at[0])
     pas_all = pas_r[:, 0, :]
     product = pas_all[0:1]
     for m in range(1, ni):
@@ -303,7 +300,7 @@
         if c == 0:
             pl.semaphore_wait(round_sem.at[1], 2)
             start(gpas_copy, nq)
-        wait(a_copy, ni, c)
+        arrived(ra.at[c, pl.ds(0, ni - 1)], a_r.at[c])
         for b in range(nb):
             total = jnp.zeros((rows_a, part_width), F32)
             for m in range(ni):
@@ -314,7 +311,7 @@
 
     def over_groups(c):
         if c == 0:
-            wait(gpas_copy, nq)
+            arrived(gpas_r.at[pl.ds(0, nq - 1)], p_r.at[0])
             every = expand_rows(gpas_r[:, 0, :])
             for n in range(nc):
                 for b in range(nb):
@@ -323,7 +320,7 @@
                     def _():
                         gexp[n] = every[:, n * width + b * part_width : n * width + (b + 1) * part_width]
 
-        wait(b_copy, nq, c)
+        arrived(rb.at[c, pl.ds(0, nq - 1)], b_r.at[c])
 
         def pass_on(k, carried):
             kb[c, k] = carried.astype(BF16)
@@ -334,7 +331,7 @@
         kr[c, pl.ds(q, 1)] = kb[c, pl.ds(q, 1)]
 
     def to_devices(c):
-        wait(k_copy, nq, c)
+        arrived(kr.at[c, pl.ds(0, nq - 1)], k_r.at[c])
         for b in range(nb):
             carried = kr[c, b * nr : (b + 1) * nr].astype(F32).reshape(rows_a, part_width)
             for m in range(ni):
@@ -344,7 +341,7 @@
         ent[c, pl.ds(i, 1)] = eb[c, pl.ds(i, 1)]
 
     def finish(c):
-        wait(e_copy, ni, c)
+        arrived(ent.at[c, pl.ds(0, ni - 1)], e_r.at[c])
         cols = slice(c * width, (c + 1) * width)
         read = jnp.dot(csel[...], ent[c].reshape(state, width), preferred_element_type=F32)
         out[:, cols] = (y[:, cols] + read * rexp[:, cols]).astype(BF16)
@@ -352,6 +349,14 @@
     for stage in (group_total, over_groups, to_devices, finish):
         for c in range(nc):
             stage(c)
+
+    arrived(pas_r.at[pl.ds(0, ni - 1)], q_s.at[0])
+    arrived(gpas_r.at[pl.ds(0, nq - 1)], p_s.at[0])
+    for c in range(nc):
+        arrived(st.at[c, pl.ds(0, ni - 1)], a_s.at[c])
+        arrived(gs.at[c, pl.ds(0, nq - 1)], b_s.at[c])
+        arrived(kb.at[c, pl.ds(0, nq - 1)], k_s.at[c])
+        arrived(eb.at[c, pl.ds(0, ni - 1)], e_s.at[c])
 
 
 def on_device(nx, ni, nr, nc, *args):
@@ -404,8 +409,8 @@
         vmem((8, chans), F32),
         vmem((nc, nq, part_width), F32),
         dma((len(operands),)),
-        *[dma((nc, n)) for n in (ni, nq, nq, ni) for _ in range(2)],
-        *[dma((n,)) for n in (ni, nq, 3) for _ in range(2)],
+        *[dma((nc,)) for _ in range(8)],
+        *[dma((n,)) for n in (1, 1, 3) for _ in range(2)],
         pltpu.SemaphoreType.REGULAR((2,)),
     ]
     return pl.pallas_call(
@@ -420,7 +425,7 @@
     )(*operands)
 
 
-def solution(mesh, nx=4, ni=4, nr=4, nc=2):
+def solution(mesh, nx=4, ni=4, nr=8, nc=4):
     return jax.shard_map(
         functools.partial(on_device, nx, ni, nr, nc),
         mesh=mesh,

time: 64.8 us -> 61.6 us (0.951)
  the two profiles are of different devices: /device:TPU:8 before, /device:TPU:1 now
where the time goes in v3:
time: 61.6 us; the launch traced here: 61.5 us
  Pallas kernels  59.6 us (97%)
  local copies, waits for them, and re-layouts  1.87 us (3%)
    pallas_call x1, Pallas kernels, on_device(): pl.pallas_call(functools.partial(kernel, nx, ni, nr, nc), out_shape=jax.S...  59.6 us
    unnamed x1, local copies, waits for them, and re-layouts  1.87 us

profile of v3, /device:TPU:1, one launch (start us, length us, event | category | flops | bytes accessed | tf_op | source)
XLA Modules:
  0.0 61.5 jit_solution(9601550329585940585)
XLA Ops:
  0.0 59.6 %shard_map.109 = bf16[256,1024]{1,0:T(8,128)(2,1)} custom-call(bf16[256,1024]{1,0:T(8,128)(2,1)} %xin.1, bf16[256,256]{1,0:T(8,128)(2,1)} %bcin_h.1, f32[4,1024]{1,0:T(4,128)} %taps_h.1, f32[1,1024]{1,0:T(1,128)} %bitcast.6, f32[4,256]{1,0:T(4,128)} %bct_h.1, f32[1,256]{1,0:T(1,128)} %bitcast.7, f32[16,256]{1,0:T(8,128)} %step_h.1, f32[1,16]{1,0:T(1,128)} %bitcast.9, ...), custom_call_target="tpu_custom_call" | custom-call | tf_op jit(solution)/shard_map/pallas_call | solution.py:416
  59.6 1.9 %copy.13 = bf16[256,1024]{1,0:T(8,128)(2,1)} copy(bf16[256,1024]{1,0:T(8,128)(2,1)} %shard_map.109) | data formatting | bytes 1048576

commit v4 on v3

--- a/solution.py
+++ b/solution.py
@@ -110,7 +110,7 @@
         return pltpu.make_async_remote_copy(src, dst, send, recv, device_id=device_id, device_id_type=MESH)
 
     def halo_copy(which):
-        src = (xin, bcin_h)[which].at[pl.ds(tok - 16, 16), :]
+        src = (xin, bcin_h)[which].at[pl.ds(tok - 8, 8), :]
         return remote(src, (xhalo, bchalo)[which], h_s.at[which], h_r.at[which], (nxt, head))
 
     def partner_copy():
@@ -172,7 +172,7 @@
 
     pick = iota((heads, LANES), 0) == iota((heads, LANES), 1)
     as_row = jnp.sum(jnp.where(pick, jnp.broadcast_to(passing, (heads, LANES)), 0.0), axis=0, keepdims=True)
-    pas_s[...] = jnp.broadcast_to(as_row, (8, LANES))
+    pas_s[...] = as_row
 
     spread = (lax.rem(iota((3 * heads, chans), 0), heads) == iota((3 * heads, chans), 1) // HEADDIM).astype(BF16)
 
@@ -214,7 +214,7 @@
     loads[9].wait()
     xfb[pl.ds(8, tok), :] = bcin[...].astype(F32)
     halo_copy(1).wait()
-    xfb[pl.ds(0, 8), :] = bchalo[...].astype(F32)[8:16]
+    xfb[pl.ds(0, 8), :] = bchalo[...].astype(F32)
     for n in range(state // LANES):
         cols = slice(n * LANES, (n + 1) * LANES)
         acc = jnp.broadcast_to(bcb[:, cols], (tok, LANES))
@@ -225,7 +225,7 @@
     partner_copy().start()
 
     halo_copy(0).wait()
-    xf[pl.ds(0, 8), :] = xhalo[...].astype(F32)[8:16]
+    xf[pl.ds(0, 8), :] = xhalo[...].astype(F32)
     acc = jnp.broadcast_to(bias[...], (16, chans))
     off_top = offb[0:16, 0:1]
     for lag in range(4):
@@ -255,7 +255,7 @@
     product = pas_all[0:1]
     for m in range(1, ni):
         product = product * pas_all[m : m + 1]
-    gpas_s[...] = jnp.broadcast_to(product, (8, LANES))
+    gpas_s[...] = product
     gpas_r[pl.ds(q, 1)] = gpas_s[...][None]
 
     spread_l = (iota((LANES, chans), 0) == iota((LANES, chans), 1) // HEADDIM).astype(BF16)
@@ -386,8 +386,8 @@
         vmem((heads, tok), F32),
         vmem((heads, tok), F32),
         vmem((1, chans), F32),
-        vmem((16, chans), BF16),
-        vmem((16, state), BF16),
+        vmem((8, chans), BF16),
+        vmem((8, state), BF16),
         vmem((tok, state), BF16),
         vmem((tok, state), BF16),
         vmem((tok, state), BF16),
@@ -402,10 +402,10 @@
         vmem((nc, nq, rows_b, part_width), BF16),
         vmem((nc, ni, rows_a, width), BF16),
         vmem((nc, ni, rows_a, width), BF16),
-        vmem((8, LANES), F32),
-        vmem((8, 8, LANES), F32),
-        vmem((8, LANES), F32),
-        vmem((nq, 8, LANES), F32),
+        vmem((1, LANES), F32),
+        vmem((8, 1, LANES), F32),
+        vmem((1, LANES), F32),
+        vmem((nq, 1, LANES), F32),
         vmem((8, chans), F32),
         vmem((nc, nq, part_width), F32),
         dma((len(operands),)),
@@ -420,9 +420,9 @@
         out_specs=pl.BlockSpec(memory_space=pltpu.VMEM),
         scratch_shapes=scratch,
         compiler_params=pltpu.CompilerParams(
-            collective_id=0, has_side_effects=True, vmem_limit_bytes=56 << 20
+            collective_id=0, has_side_effects=True, vmem_limit_bytes=48 << 20
         ),
-    )(*operands)
+    )(*[pltpu.with_memory_space_constraint(a, pltpu.HBM) for a in operands])
 
 
 def solution(mesh, nx=4, ni=4, nr=8, nc=4):

time: 61.6 us -> 57.2 us (0.929)
  Pallas kernels: 59.6 us -> 56.3 us
  local copies, waits for them, and re-layouts: 1.87 us -> 0.8 us
    pallas_call x1, Pallas kernels: 59.6 us -> 56.3 us  [on_device(): pl.pallas_call(functools.partial(kernel, nx, ni, nr, nc), out_shape=jax.S...]
    unnamed x1, local copies, waits for them, and re-layouts: 1.87 us -> 0.8 us
where the time goes in v4:
time: 57.2 us; the launch traced here: 57.1 us
  Pallas kernels  56.3 us (98%)
  local copies, waits for them, and re-layouts  0.8 us (1%)
    pallas_call x1, Pallas kernels, on_device(): pl.pallas_call(functools.partial(kernel, nx, ni, nr, nc), out_shape=jax.S...  56.3 us

profile of v4, /device:TPU:1, one launch (start us, length us, event | category | flops | bytes accessed | tf_op | source)
XLA Modules:
  0.0 57.1 jit_solution(14246964320868624996)
XLA Ops:
  0.0 56.3 %shard_map.109 = bf16[256,1024]{1,0:T(8,128)(2,1)S(1)} custom-call(bf16[256,1024]{1,0:T(8,128)(2,1)} %xin.1, bf16[256,256]{1,0:T(8,128)(2,1)} %bcin_h.1, f32[4,1024]{1,0:T(4,128)} %taps_h.1, f32[1,1024]{1,0:T(1,128)} %bitcast.6, f32[4,256]{1,0:T(4,128)} %bct_h.1, f32[1,256]{1,0:T(1,128)} %bitcast.7, f32[16,256]{1,0:T(8,128)} %step_h.1, f32[1,16]{1,0:T(1,128)} %bitcast.9, ...), custom_call_target="tpu_custom_call" | custom-call | tf_op jit(solution)/shard_map/pallas_call | solution.py:416
  56.3 0.8 %copy.13 = bf16[256,1024]{1,0:T(8,128)(2,1)} copy(bf16[256,1024]{1,0:T(8,128)(2,1)S(1)} %shard_map.109) | data formatting | bytes 1048576

commit v5 on v4

--- a/solution.py
+++ b/solution.py
@@ -113,8 +113,9 @@
         src = (xin, bcin_h)[which].at[pl.ds(tok - 8, 8), :]
         return remote(src, (xhalo, bchalo)[which], h_s.at[which], h_r.at[which], (nxt, head))
 
-    def partner_copy():
-        return remote(bown, bother, h_s.at[2], h_r.at[2], (s, partner))
+    def partner_copy(which):
+        at = (pl.ds(0, 16), pl.ds(16, tok - 16))[which]
+        return remote(bown.at[at, :], bother.at[at, :], h_s.at[2 + which], h_r.at[2 + which], (s, partner))
 
     def pas_copy(d):
         return remote(pas_s, pas_r.at[i], q_s.at[0], q_r.at[0], device(q, member(d)))
@@ -181,9 +182,6 @@
             jnp.concatenate(split3(value), axis=0), spread, (((0,), (0,)), ((), ())), preferred_element_type=F32
         )
 
-    sexp[...] = expand(s_row)
-    rexp[...] = expand(rate_row)
-
     for load in loads[5:8]:
         load.wait()
 
@@ -197,32 +195,40 @@
             acc = acc + (term if lag == 0 else jnp.where(offb[...] >= lag, term, 0.0))
         xc[:, cols] = silu(acc).astype(BF16)
 
+    for load in (loads[4], *loads[8:10]):
+        load.wait()
+    xfb[pl.ds(8, tok), :] = bcin[...].astype(F32)
+
+    def conv_bc(rows):
+        for n in range(state // LANES):
+            cols = slice(n * LANES, (n + 1) * LANES)
+            acc = jnp.broadcast_to(bcb[:, cols], (rows, LANES))
+            for lag in range(4):
+                term = bct[3 - lag : 4 - lag, cols] * xfb[pl.ds(8 - lag, rows), cols]
+                acc = acc + (term if lag == 0 else jnp.where(offb[0:rows] >= lag, term, 0.0))
+            bown[0:rows, cols] = silu(acc).astype(BF16)
+
+    conv_bc(tok)
     pl.semaphore_wait(barrier, (ni - 1) + (nx - 1) + 5)
     halo_copy(1).start()
     halo_copy(0).start()
+    partner_copy(1).start()
     tell(0)
     pas_r[pl.ds(i, 1)] = pas_s[...][None]
     start(pas_copy, ni)
+
+    sexp[...] = expand(s_row)
+    rexp[...] = expand(rate_row)
 
     @pl.loop(0, chans // LANES)
     def _(n):
         cols = pl.ds(pl.multiple_of(n * LANES, LANES), LANES)
         xs[:, cols] = (xc[:, cols].astype(F32) * sexp[:, cols]).astype(BF16)
 
-    loads[4].wait()
-    loads[8].wait()
-    loads[9].wait()
-    xfb[pl.ds(8, tok), :] = bcin[...].astype(F32)
     halo_copy(1).wait()
     xfb[pl.ds(0, 8), :] = bchalo[...].astype(F32)
-    for n in range(state // LANES):
-        cols = slice(n * LANES, (n + 1) * LANES)
-        acc = jnp.broadcast_to(bcb[:, cols], (tok, LANES))
-        for lag in range(4):
-            term = bct[3 - lag : 4 - lag, cols] * xfb[pl.ds(8 - lag, tok), cols]
-            acc = acc + (term if lag == 0 else jnp.where(offb[...] >= lag, term, 0.0))
-        bown[:, cols] = silu(acc).astype(BF16)
-    partner_copy().start()
+    conv_bc(16)
+    partner_copy(0).start()
 
     halo_copy(0).wait()
     xf[pl.ds(0, 8), :] = xhalo[...].astype(F32)
@@ -235,7 +241,8 @@
     xc[0:16, :] = top
     xs[0:16, :] = (top.astype(F32) * sexp[0:16, :]).astype(BF16)
 
-    partner_copy().wait()
+    partner_copy(0).wait()
+    partner_copy(1).wait()
     even = odd == 0
     bsel[...] = jnp.where(even, bown[...], bother[...])
     csel[...] = jnp.where(even, bother[...], bown[...])
@@ -410,7 +417,7 @@
         vmem((nc, nq, part_width), F32),
         dma((len(operands),)),
         *[dma((nc,)) for _ in range(8)],
-        *[dma((n,)) for n in (1, 1, 3) for _ in range(2)],
+        *[dma((n,)) for n in (1, 1, 4) for _ in range(2)],
         pltpu.SemaphoreType.REGULAR((2,)),
     ]
     return pl.pallas_call(

time: 57.2 us -> 56.3 us (0.984)
  Pallas kernels: 56.3 us -> 55.4 us
    pallas_call x1, Pallas kernels: 56.3 us -> 55.4 us  [on_device(): pl.pallas_call(functools.partial(kernel, nx, ni, nr, nc), out_shape=jax.S...]
where the time goes in v5:
time: 56.3 us; the launch traced here: 56.2 us
  Pallas kernels  55.4 us (98%)
  local copies, waits for them, and re-layouts  0.8 us (1%)
    pallas_call x1, Pallas kernels, on_device(): pl.pallas_call(functools.partial(kernel, nx, ni, nr, nc), out_shape=jax.S...  55.4 us

profile of v5, /device:TPU:1, one launch (start us, length us, event | category | flops | bytes accessed | tf_op | source)
XLA Modules:
  0.0 56.2 jit_solution(18396261798037608790)
XLA Ops:
  0.0 55.4 %shard_map.109 = bf16[256,1024]{1,0:T(8,128)(2,1)S(1)} custom-call(bf16[256,1024]{1,0:T(8,128)(2,1)} %xin.1, bf16[256,256]{1,0:T(8,128)(2,1)} %bcin_h.1, f32[4,1024]{1,0:T(4,128)} %taps_h.1, f32[1,1024]{1,0:T(1,128)} %bitcast.6, f32[4,256]{1,0:T(4,128)} %bct_h.1, f32[1,256]{1,0:T(1,128)} %bitcast.7, f32[16,256]{1,0:T(8,128)} %step_h.1, f32[1,16]{1,0:T(1,128)} %bitcast.9, ...), custom_call_target="tpu_custom_call" | custom-call | tf_op jit(solution)/shard_map/pallas_call | solution.py:423
  55.4 0.8 %copy.13 = bf16[256,1024]{1,0:T(8,128)(2,1)} copy(bf16[256,1024]{1,0:T(8,128)(2,1)S(1)} %shard_map.109) | data formatting | bytes 1048576

commit v6 on v5

--- a/solution.py
+++ b/solution.py
@@ -35,7 +35,7 @@
     xin, bcin_h, taps_h, bias_h, bct_h, bcb_h, step_h, sbias_h, dlog_h, sgain_h, off_h,
     out,
     xv, bcin, taps, bias, bct, bcb, step, sbias, dlog, sgain, off,
-    xf, xfb, xc, offb, sexp, xs, rexp, rate, td, skip, xhalo, bchalo, bown, bother, bsel, csel,
+    xf, xfb, xc, offb, sexp, xs, rexp, rate, td, skip, xhalo, bchalo, bown, bother, bsel, csel, bturned,
     smask, y, st, ra, gs, rb, kb, kr, eb, ent, pas_s, pas_r, gpas_s, gpas_r, pexp, gexp,
     ins, a_s, a_r, b_s, b_r, k_s, k_r, e_s, e_r, q_s, q_r, p_s, p_r, h_s, h_r, round_sem,
 ):
@@ -244,12 +244,14 @@
     partner_copy(0).wait()
     partner_copy(1).wait()
     even = odd == 0
-    bsel[...] = jnp.where(even, bown[...], bother[...])
+    b_rows = jnp.where(even, bown[...], bother[...])
+    bsel[...] = b_rows
+    bturned[...] = b_rows.T
     csel[...] = jnp.where(even, bother[...], bown[...])
 
     for c in range(nc):
         cols = slice(c * width, (c + 1) * width)
-        block_state = lax.dot_general(bsel[...], xs[:, cols], (((0,), (0,)), ((), ())), preferred_element_type=F32)
+        block_state = jnp.dot(bturned[...], xs[:, cols], preferred_element_type=F32)
         st[c] = block_state.astype(BF16).reshape(ni, rows_a, width)
         start(a_copy, ni, c)
         ra[c, pl.ds(i, 1)] = st[c, pl.ds(i, 1)]
@@ -399,6 +401,7 @@
         vmem((tok, state), BF16),
         vmem((tok, state), BF16),
         vmem((tok, state), BF16),
+        vmem((state, tok), BF16),
         vmem((tok, tok), F32),
         vmem((tok, chans), F32),
         vmem((nc, ni, rows_a, width), BF16),

time: 56.3 us -> 56.3 us (level)
  no operation moved by 1% of the time
where the time goes in v6:
time: 56.3 us; the launch traced here: 56.2 us
  Pallas kernels  55.4 us (98%)
  local copies, waits for them, and re-layouts  0.8 us (1%)
    pallas_call x1, Pallas kernels, on_device(): pl.pallas_call(functools.partial(kernel, nx, ni, nr, nc), out_shape=jax.S...  55.4 us

profile of v6, /device:TPU:1, one launch (start us, length us, event | category | flops | bytes accessed | tf_op | source)
XLA Modules:
  0.0 56.2 jit_solution(10069812558592958907)
XLA Ops:
  0.0 55.4 %shard_map.109 = bf16[256,1024]{1,0:T(8,128)(2,1)S(1)} custom-call(bf16[256,1024]{1,0:T(8,128)(2,1)} %xin.1, bf16[256,256]{1,0:T(8,128)(2,1)} %bcin_h.1, f32[4,1024]{1,0:T(4,128)} %taps_h.1, f32[1,1024]{1,0:T(1,128)} %bitcast.6, f32[4,256]{1,0:T(4,128)} %bct_h.1, f32[1,256]{1,0:T(1,128)} %bitcast.7, f32[16,256]{1,0:T(8,128)} %step_h.1, f32[1,16]{1,0:T(1,128)} %bitcast.9, ...), custom_call_target="tpu_custom_call" | custom-call | tf_op jit(solution)/shard_map/pallas_call | solution.py:426
  55.4 0.8 %copy.13 = bf16[256,1024]{1,0:T(8,128)(2,1)} copy(bf16[256,1024]{1,0:T(8,128)(2,1)S(1)} %shard_map.109) | data formatting | bytes 1048576
